TPU v7x, 256 devices: a whole 4x4x8 slice. The times are simulated.
256 devices in a mesh: user: 16 (over x, y_hi, core), item: 16 (over z, y_lo).
Axes of the slice: x: 4, y: 4 (y_hi: 2, y_lo: 2; y = y_hi * 2 + y_lo), z: 8, core: 2. Of those that a mesh axis runs over, the one named last changes fastest.
Arguments:
- item_factors: float32 [16, 4096, 128], P('item', 'user'), may hold values from -2 to 2
- weights: float32 [128, 256, 128, 128], P('user', 'item'), may hold values from 0 to 100
- tile_ids: int32 [128, 16, 16], P('user', 'item'), may hold values from 0 to 31, as said below
- start_factors: float32 [16384, 128], P('user'), may hold values from -4 to 4
Outputs:
- user_factors: float32 [16384, 128], P('user')
Inputs may be any that keep to these rules, and one draw needn't show every extreme that they name: `tile_ids`: entries of one user block and item block are distinct.
All inputs are finite; a program needn't handle non-finite values.
Results may differ from a plain program's by a relative error of at most 0.0003.
Values sent between devices are 32-bit elements; how exact they have to be, the bound alone decides.
A program may use at most 64 MiB of HBM per device.

v0:
```python
import jax
import jax.numpy as jnp
from jax import lax
from jax.sharding import PartitionSpec as P

ITERS = 3
HIGH = lax.Precision.HIGHEST


def partial_image(chosen, wtiles, vectors):
    blocks, count, tile, rank = chosen.shape
    shaped = vectors.reshape(blocks, tile, rank)
    scores = jnp.einsum("bkjr,bur->bkuj", chosen, shaped, precision=HIGH)
    back = jnp.einsum("bkuj,bkjr->bur", scores * wtiles, chosen, precision=HIGH)
    return back.reshape(blocks * tile, rank)


def local_terms(vectors, gram):
    return (
        jnp.dot(vectors, gram, preferred_element_type=jnp.float32, precision=HIGH) + 1.0 * vectors
    )


def update(state, image):
    solved, resid, direction, norm_now = state
    alpha = norm_now / (jnp.sum(direction * image, axis=1, keepdims=True) + 1e-06)
    solved = solved + alpha * direction
    resid = resid - alpha * image
    norm_next = jnp.sum(resid * resid, axis=1, keepdims=True)
    direction = resid + norm_next / (norm_now + 1e-06) * direction
    return (solved, resid, direction, norm_next)


def local(item_factors, weights, tile_ids, start_factors):
    slab = item_factors[0]
    rank = slab.shape[1]
    tile = weights.shape[2]
    gram = lax.psum(
        jnp.dot(slab.T, slab, preferred_element_type=jnp.float32, precision=HIGH), ("user", "item")
    )
    block = lax.all_gather(slab, "user", axis=0, tiled=True)
    vtiles = block.reshape(-1, tile, rank)
    chosen = jnp.take(vtiles, tile_ids[:, 0, :], axis=0)
    blocks = chosen.shape[0]
    prefs = jnp.where(weights > 0, 1.0 + weights, 0.0)
    rhs_part = jnp.einsum("bkuj,bkjr->bur", prefs, chosen, precision=HIGH).reshape(
        blocks * tile, rank
    )
    start_part = partial_image(chosen, weights, start_factors)
    rhs, image = lax.psum((rhs_part, start_part), "item")
    resid = rhs - image - local_terms(start_factors, gram)
    norm_now = jnp.sum(resid * resid, axis=1, keepdims=True)
    state = (start_factors, resid, resid, norm_now)
    for step in range(ITERS):
        direction = state[2]
        image = lax.psum(partial_image(chosen, weights, direction), "item")
        state = update(state, image + local_terms(direction, gram))
    return state[0]


def solution(mesh):
    in_specs = (
        P("item", "user", None),
        P("user", "item", None, None),
        P("user", "item", None),
        P("user", None),
    )
    out_specs = P("user", None)
    return jax.shard_map(local, mesh=mesh, in_specs=in_specs, out_specs=out_specs, check_vma=False)
```

profile of v0, /device:TPU:2, one launch (start us, length us, event | category | flops | bytes accessed | tf_op | source)
XLA Modules:
  0.0 901.7 jit_solution(9021807846128946891)
XLA Ops:
  8.1 2.0 fusion.48
  11.7 55.4 %all-gather.3.cloned.1.call-done = f32[1,4096,128]{2,1,0:T(8,128)} async-done(((f32[1,256,128]{2,1,0:T(8,128)}), f32[1,4096,128]{2,1,0:T(8,128)}) %all-gather.3.cloned.1.call-update) | async-done | bytes 2097168 | tf_op jit(solution)/shard_map/all_gather | solution.py:41
  67.0 6.0 gather_fusion
  73.0 11.9 %fusion.18 = f32[8,16,128,128]{2,3,1,0:T(8,128)S(1)} fusion(f32[8,128,128,1]{2,1,3,0:T(8,128)S(1)} %bitcast.77, f32[8,16,128,128]{3,2,1,0:T(8,128)} %bitcast.67, pred[8,16]{1,0:T(8,128)(4,1)S(1)} %compare_and_fusion), kind=kOutput, calls=%fused_computation.23 | convolution fusion | flops 3223322624 | bytes 17301632 | tf_op jit(solution)/shard_map/bkjr,bur->bkuj/dot_general | solution.py:13
  84.9 11.5 %fusion.3 = f32[8,128,128,1]{2,1,3,0:T(8,128)S(1)} fusion(f32[8,16,128,128]{3,2,1,0:T(8,128)} %param.5, f32[8,16,128,128]{2,3,1,0:T(8,128)S(1)} %fusion.18, f32[8,16,128,128]{3,2,1,0:T(8,128)S(1)} %bitcast.74, pred[8,16]{1,0:T(8,128)(4,1)S(1)} %compare_and_fusion), kind=kOutput, calls=%fused_computation.8 | convolution fusion | flops 3225419776 | bytes 25690240 | tf_op jit(solution)/shard_map/bkuj,bkjr->bur/dot_general | solution.py:14
  96.4 12.2 %fusion.4 = f32[8,128,128,1]{2,1,3,0:T(8,128)S(1)} fusion(f32[8,16,128,128]{3,2,1,0:T(8,128)} %param.5, f32[8,16,128,128]{3,2,1,0:T(8,128)S(1)} %bitcast.75, pred[8,16]{1,0:T(8,128)(4,1)S(1)} %compare_and_fusion), kind=kOutput, calls=%fused_computation.9 | convolution fusion | flops 3229614080 | bytes 17301632 | tf_op jit(solution)/shard_map/bkuj,bkjr->bur/dot_general | solution.py:46
  108.6 1.0 copy.5
  110.9 147.4 %all-reduce.7.cloned.1.call-done = f32[128,128]{1,0:T(8,128)} async-done(((f32[128,128]{1,0:T(8,128)}), f32[128,128]{1,0:T(8,128)}) %all-reduce.7.cloned.1.call-update) | async-done | bytes 65552 | tf_op jit(solution)/shard_map/psum | solution.py:38
  258.2 139.7 %all-reduce.15.cloned.1.call-done = (f32[1024,128]{0,1:T(8,128)}, f32[1024,128]{0,1:T(8,128)}) async-done(((f32[1024,128]{0,1:T(8,128)}, f32[1024,128]{0,1:T(8,128)}), (f32[1024,128]{0,1:T(8,128)}, f32[1024,128]{0,1:T(8,128)})) %all-reduce.15.cloned.1.call-update) | async-done | bytes 1048592 | tf_op jit(solution)/shard_map/psum | solution.py:50
  397.9 1.9 fusion.42
  400.1 10.3 %fusion.15 = f32[8,128,16,128]{3,1,2,0:T(8,128)S(1)} fusion(f32[8,128,128,1]{2,1,3,0:T(8,128)S(1)} %bitcast.83, f32[8,16,128,128]{3,2,1,0:T(8,128)} %bitcast.68, pred[8,16]{1,0:T(8,128)(4,1)S(1)} %compare_and_fusion), kind=kOutput, calls=%fused_computation.20 | convolution fusion | flops 3223322624 | bytes 17301632 | tf_op jit(solution)/shard_map/bkjr,bur->bkuj/dot_general | solution.py:13
  410.4 12.8 %fusion.2 = f32[8,128,128,1]{2,1,3,0:T(8,128)S(1)} fusion(f32[8,16,128,128]{3,2,1,0:T(8,128)} %param.5, f32[8,128,16,128]{3,1,2,0:T(8,128)S(1)} %fusion.15, f32[8,16,128,128]{3,2,1,0:T(8,128)} %bitcast.69, pred[8,16]{1,0:T(8,128)(4,1)S(1)} %compare_and_fusion), kind=kOutput, calls=%fused_computation.6 | convolution fusion | flops 3225419776 | bytes 25690240 | tf_op jit(solution)/shard_map/bkuj,bkjr->bur/dot_general | solution.py:14
  423.2 1.0 copy.27
  424.3 138.1 %all-reduce.9.cloned.1.call-done = f32[1024,128]{0,1:T(8,128)} async-done(((f32[1024,128]{0,1:T(8,128)}), f32[1024,128]{0,1:T(8,128)}) %all-reduce.9.cloned.1.call-update) | async-done | bytes 524304 | tf_op jit(solution)/shard_map/psum | solution.py:56
  562.4 1.7 multiply_reduce_fusion.3
  564.5 10.4 %fusion.12 = f32[8,128,16,128]{3,1,2,0:T(8,128)S(1)} fusion(f32[8,128,128,1]{2,1,3,0:T(8,128)S(1)} %bitcast.84, f32[8,16,128,128]{3,2,1,0:T(8,128)} %bitcast.70, pred[8,16]{1,0:T(8,128)(4,1)S(1)} %compare_and_fusion), kind=kOutput, calls=%fused_computation.17 | convolution fusion | flops 3223322624 | bytes 17301632 | tf_op jit(solution)/shard_map/bkjr,bur->bkuj/dot_general | solution.py:13
  574.9 12.7 %fusion.1 = f32[8,128,128,1]{2,1,3,0:T(8,128)S(1)} fusion(f32[8,16,128,128]{3,2,1,0:T(8,128)} %param.5, f32[8,128,16,128]{3,1,2,0:T(8,128)S(1)} %fusion.12, f32[8,16,128,128]{3,2,1,0:T(8,128)} %bitcast.71, pred[8,16]{1,0:T(8,128)(4,1)S(1)} %compare_and_fusion), kind=kOutput, calls=%fused_computation.4 | convolution fusion | flops 3225419776 | bytes 25690240 | tf_op jit(solution)/shard_map/bkuj,bkjr->bur/dot_general | solution.py:14
  587.6 1.0 copy.29
  588.7 137.8 %all-reduce.11.cloned.1.call-done = f32[1024,128]{0,1:T(8,128)} async-done(((f32[1024,128]{0,1:T(8,128)}), f32[1024,128]{0,1:T(8,128)}) %all-reduce.11.cloned.1.call-update) | async-done | bytes 524304 | tf_op jit(solution)/shard_map/psum | solution.py:56
  726.5 1.7 multiply_reduce_fusion.1
  728.7 10.4 %fusion.9 = f32[8,128,16,128]{3,1,2,0:T(8,128)S(1)} fusion(f32[8,128,128,1]{2,1,3,0:T(8,128)S(1)} %bitcast.85, f32[8,16,128,128]{3,2,1,0:T(8,128)} %bitcast.72, pred[8,16]{1,0:T(8,128)(4,1)S(1)} %compare_and_fusion), kind=kOutput, calls=%fused_computation.14 | convolution fusion | flops 3223322624 | bytes 17301632 | tf_op jit(solution)/shard_map/bkjr,bur->bkuj/dot_general | solution.py:13
  739.1 12.7 %fusion = f32[8,128,128,1]{2,1,3,0:T(8,128)S(1)} fusion(f32[8,16,128,128]{3,2,1,0:T(8,128)} %param.5, f32[8,128,16,128]{3,1,2,0:T(8,128)S(1)} %fusion.9, f32[8,16,128,128]{3,2,1,0:T(8,128)} %bitcast.73, pred[8,16]{1,0:T(8,128)(4,1)S(1)} %compare_and_fusion), kind=kOutput, calls=%fused_computation.2 | convolution fusion | flops 3225419776 | bytes 25690240 | tf_op jit(solution)/shard_map/bkuj,bkjr->bur/dot_general | solution.py:14
  752.9 137.9 %all-reduce.13.cloned.1.call-done = f32[1024,128]{0,1:T(8,128)} async-done(((f32[1024,128]{0,1:T(8,128)}), f32[1024,128]{0,1:T(8,128)}) %all-reduce.13.cloned.1.call-update) | async-done | bytes 524304 | tf_op jit(solution)/shard_map/psum | solution.py:56
  890.7 1.7 fusion.47
  (39 shorter events, 6.9 us)
Async XLA Ops:
  7.4 59.7 %all-gather.3.cloned.1.call-start = ((), (), s32[]{:S(2)}) async-start(), calls=%async_computation.4 | async-start | bytes 2228224 | tf_op jit(solution)/shard_map/all_gather | solution.py:41
  8.1 250.1 %all-reduce.7.cloned.1.call-start = ((), (), s32[]{:S(2)}) async-start(), calls=%async_computation | async-start | bytes 131072 | tf_op jit(solution)/shard_map/psum | solution.py:38
  10.2 387.8 %all-reduce.15.cloned.1.call-start = ((), (), s32[]{:S(2)}) async-start(), calls=%async_computation.5 | async-start | bytes 2097152 | tf_op jit(solution)/shard_map/psum | solution.py:50
  67.0 6.0 copy-start.1
  73.0 11.9 %copy-start = (f32[128,128,128]{2,1,0:T(8,128)S(1)}, f32[128,128,128]{2,1,0:T(8,128)}, u32[]{:S(2)}) copy-start(f32[128,128,128]{2,1,0:T(8,128)} %gather_fusion) | copy-start | bytes 25165828
  110.6 451.8 %all-reduce.9.cloned.1.call-start = ((), (), s32[]{:S(2)}) async-start(), calls=%async_computation.1 | async-start | bytes 1048576 | tf_op jit(solution)/shard_map/psum | solution.py:56
  410.4 151.9 %copy-start.2 = (f32[128,128]{1,0:T(8,128)S(1)}, f32[128,128]{1,0:T(8,128)}, u32[]{:S(2)}) copy-start(f32[128,128]{1,0:T(8,128)} %all-reduce.7.cloned.1.call-done) | copy-start | bytes 196612
  424.2 302.3 %all-reduce.11.cloned.1.call-start = ((), (), s32[]{:S(2)}) async-start(), calls=%async_computation.2 | async-start | bytes 1048576 | tf_op jit(solution)/shard_map/psum | solution.py:56
  588.7 302.1 %all-reduce.13.cloned.1.call-start = ((), (), s32[]{:S(2)}) async-start(), calls=%async_computation.3 | async-start | bytes 1048576 | tf_op jit(solution)/shard_map/psum | solution.py:56
Sparse Core Ops, SparseCore 0:
  10.8 56.1 all-gather.2
Sparse Core Ops, SparseCore 1:
  14.1 244.1 all-reduce.6
  260.8 137.1 all-reduce.14
  424.3 138.0 all-reduce.8
  588.7 137.7 all-reduce.10
  753.0 137.7 all-reduce.12
where the time goes:
time: 909 us; the launch traced here: 902 us
  waiting for transfers between devices  757 us (83%)
  matrix products  114 us (13%)
  between operations  15.7 us (2%)
  local copies, waits for them, and re-layouts  12.8 us (1%)
    psum x3, waiting for transfers between devices, local(): image = lax.psum(partial_image(chosen, weights, direction), 'item')  414 us
    psum x1, waiting for transfers between devices, local(): lax.psum(jnp.dot(slab.T, slab, preferred_element_type=jnp.float32, precis...  147 us
    psum x1, waiting for transfers between devices, local(): rhs, image = lax.psum((rhs_part, start_part), 'item')  140 us
    all_gather x1, waiting for transfers between devices, local(): block = lax.all_gather(slab, 'user', axis=0, tiled=True)  55.4 us
    dot_general x4, matrix products, partial_image(): back = jnp.einsum('bkuj,bkjr->bur', scores * wtiles, chosen, precision=HIGH)  49.7 us
    dot_general x4, matrix products, partial_image(): scores = jnp.einsum('bkjr,bur->bkuj', chosen, shaped, precision=HIGH)  43 us
  transfers between devices with their start and end apart: 6, of which 6 were waited for; matrix products, arithmetic and copies ran while one was open for 5% of the time, Pallas kernels for 0%

commit v1 on v0

--- a/solution.py
+++ b/solution.py
@@ -35,9 +35,9 @@
     slab = item_factors[0]
     rank = slab.shape[1]
     tile = weights.shape[2]
-    gram = lax.psum(
-        jnp.dot(slab.T, slab, preferred_element_type=jnp.float32, precision=HIGH), ("user", "item")
-    )
+    gram = jnp.dot(slab.T, slab, preferred_element_type=jnp.float32, precision=HIGH)
+    for k in ("user", "item"):
+        gram = lax.psum(gram, k)
     block = lax.all_gather(slab, "user", axis=0, tiled=True)
     vtiles = block.reshape(-1, tile, rank)
     chosen = jnp.take(vtiles, tile_ids[:, 0, :], axis=0)

time: 909 us -> 855 us (0.941)
  waiting for transfers between devices: 757 us -> 704 us
    psum x2, waiting for transfers between devices: 287 us -> 234 us  [local(): gram = lax.psum(gram, k)]
  transfers between devices with their start and end apart: 6 -> 6, of which waited for: 6 -> 6; matrix products, arithmetic and copies ran while one was open for 5% -> 6% of each run, Pallas kernels for 0% -> 0%
where the time goes in v1:
time: 855 us; the launch traced here: 847 us
  waiting for transfers between devices  704 us (82%)
  matrix products  114 us (13%)
  between operations  13.9 us (2%)
  local copies, waits for them, and re-layouts  12.8 us (1%)
    psum x3, waiting for transfers between devices, local(): image = lax.psum(partial_image(chosen, weights, direction), 'item')  414 us
    psum x2, waiting for transfers between devices, local(): gram = lax.psum(gram, k)  234 us
    all_gather x1, waiting for transfers between devices, local(): block = lax.all_gather(slab, 'user', axis=0, tiled=True)  55.3 us
    dot_general x4, matrix products, partial_image(): back = jnp.einsum('bkuj,bkjr->bur', scores * wtiles, chosen, precision=HIGH)  49.7 us
    dot_general x4, matrix products, partial_image(): scores = jnp.einsum('bkjr,bur->bkuj', chosen, shaped, precision=HIGH)  43.3 us
  transfers between devices with their start and end apart: 6, of which 6 were waited for; matrix products, arithmetic and copies ran while one was open for 6% of the time, Pallas kernels for 0%

profile of v1, /device:TPU:2, one launch (start us, length us, event | category | flops | bytes accessed | tf_op | source)
XLA Modules:
  0.0 847.2 jit_solution(9180157162079011603)
XLA Ops:
  7.3 2.0 fusion.48
  10.8 55.3 %all-gather.3.cloned.1.call-done = f32[1,4096,128]{2,1,0:T(8,128)} async-done(((f32[1,256,128]{2,1,0:T(8,128)}), f32[1,4096,128]{2,1,0:T(8,128)}) %all-gather.3.cloned.1.call-update) | async-done | bytes 2097168 | tf_op jit(solution)/shard_map/all_gather | solution.py:41
  66.1 6.0 gather_fusion
  72.1 11.9 %fusion.18 = f32[8,16,128,128]{2,3,1,0:T(8,128)S(1)} fusion(f32[8,128,128,1]{2,1,3,0:T(8,128)S(1)} %bitcast.77, f32[8,16,128,128]{3,2,1,0:T(8,128)} %bitcast.67, pred[8,16]{1,0:T(8,128)(4,1)S(1)} %compare_and_fusion), kind=kOutput, calls=%fused_computation.23 | convolution fusion | flops 3223322624 | bytes 17301632 | tf_op jit(solution)/shard_map/bkjr,bur->bkuj/dot_general | solution.py:13
  84.0 11.5 %fusion.3 = f32[8,128,128,1]{2,1,3,0:T(8,128)S(1)} fusion(f32[8,16,128,128]{3,2,1,0:T(8,128)} %param.5, f32[8,16,128,128]{2,3,1,0:T(8,128)S(1)} %fusion.18, f32[8,16,128,128]{3,2,1,0:T(8,128)S(1)} %bitcast.74, pred[8,16]{1,0:T(8,128)(4,1)S(1)} %compare_and_fusion), kind=kOutput, calls=%fused_computation.8 | convolution fusion | flops 3225419776 | bytes 25690240 | tf_op jit(solution)/shard_map/bkuj,bkjr->bur/dot_general | solution.py:14
  95.5 12.0 %fusion.4 = f32[8,128,128,1]{2,1,3,0:T(8,128)S(1)} fusion(f32[8,16,128,128]{3,2,1,0:T(8,128)} %param.5, f32[8,16,128,128]{3,2,1,0:T(8,128)S(1)} %bitcast.75, pred[8,16]{1,0:T(8,128)(4,1)S(1)} %compare_and_fusion), kind=kOutput, calls=%fused_computation.9 | convolution fusion | flops 3229614080 | bytes 17301632 | tf_op jit(solution)/shard_map/bkuj,bkjr->bur/dot_general | solution.py:46
  107.5 1.0 copy.5
  108.5 1.0 copy.6
  109.5 89.3 %all-reduce.7.cloned.1.call-done = f32[128,128]{1,0:T(8,128)} async-done(((f32[128,128]{1,0:T(8,128)}), f32[128,128]{1,0:T(8,128)}) %all-reduce.7.cloned.1.call-update) | async-done | bytes 65552 | tf_op jit(solution)/shard_map/psum | solution.py:40
  199.1 144.8 %all-reduce.15.cloned.1.call-done = (f32[128,128]{1,0:T(8,128)}, f32[1024,128]{0,1:T(8,128)}, f32[1024,128]{0,1:T(8,128)}) async-done(((f32[128,128]{1,0:T(8,128)}, f32[1024,128]{0,1:T(8,128)}, f32[1024,128]{0,1:T(8,128)}), (f32[128,128]{1,0:T(8,128)}, f32[1024,128]{0,1:T(8,128)}, f32[1024,128]{0,1:T(8,128)})) %all-reduce.15.cloned.1.call-update) | async-done | bytes 1114128 | tf_op jit(solution)/shard_map/psum | solution.py:40
  343.9 1.9 fusion.42
  346.0 10.7 %fusion.15 = f32[8,128,16,128]{3,1,2,0:T(8,128)S(1)} fusion(f32[8,128,128,1]{2,1,3,0:T(8,128)S(1)} %bitcast.83, f32[8,16,128,128]{3,2,1,0:T(8,128)} %bitcast.68, pred[8,16]{1,0:T(8,128)(4,1)S(1)} %compare_and_fusion), kind=kOutput, calls=%fused_computation.20 | convolution fusion | flops 3223322624 | bytes 17301632 | tf_op jit(solution)/shard_map/bkjr,bur->bkuj/dot_general | solution.py:13
  356.8 12.8 %fusion.2 = f32[8,128,128,1]{2,1,3,0:T(8,128)S(1)} fusion(f32[8,16,128,128]{3,2,1,0:T(8,128)} %param.5, f32[8,128,16,128]{3,1,2,0:T(8,128)S(1)} %fusion.15, f32[8,16,128,128]{3,2,1,0:T(8,128)} %bitcast.69, pred[8,16]{1,0:T(8,128)(4,1)S(1)} %compare_and_fusion), kind=kOutput, calls=%fused_computation.6 | convolution fusion | flops 3225419776 | bytes 25690240 | tf_op jit(solution)/shard_map/bkuj,bkjr->bur/dot_general | solution.py:14
  369.5 1.0 copy.27
  370.6 137.8 %all-reduce.9.cloned.1.call-done = f32[1024,128]{0,1:T(8,128)} async-done(((f32[1024,128]{0,1:T(8,128)}), f32[1024,128]{0,1:T(8,128)}) %all-reduce.9.cloned.1.call-update) | async-done | bytes 524304 | tf_op jit(solution)/shard_map/psum | solution.py:56
  508.4 1.7 multiply_reduce_fusion.3
  510.5 10.3 %fusion.12 = f32[8,128,16,128]{3,1,2,0:T(8,128)S(1)} fusion(f32[8,128,128,1]{2,1,3,0:T(8,128)S(1)} %bitcast.84, f32[8,16,128,128]{3,2,1,0:T(8,128)} %bitcast.70, pred[8,16]{1,0:T(8,128)(4,1)S(1)} %compare_and_fusion), kind=kOutput, calls=%fused_computation.17 | convolution fusion | flops 3223322624 | bytes 17301632 | tf_op jit(solution)/shard_map/bkjr,bur->bkuj/dot_general | solution.py:13
  520.9 12.7 %fusion.1 = f32[8,128,128,1]{2,1,3,0:T(8,128)S(1)} fusion(f32[8,16,128,128]{3,2,1,0:T(8,128)} %param.5, f32[8,128,16,128]{3,1,2,0:T(8,128)S(1)} %fusion.12, f32[8,16,128,128]{3,2,1,0:T(8,128)} %bitcast.71, pred[8,16]{1,0:T(8,128)(4,1)S(1)} %compare_and_fusion), kind=kOutput, calls=%fused_computation.4 | convolution fusion | flops 3225419776 | bytes 25690240 | tf_op jit(solution)/shard_map/bkuj,bkjr->bur/dot_general | solution.py:14
  534.7 138.2 %all-reduce.11.cloned.1.call-done = f32[1024,128]{0,1:T(8,128)} async-done(((f32[1024,128]{0,1:T(8,128)}), f32[1024,128]{0,1:T(8,128)}) %all-reduce.11.cloned.1.call-update) | async-done | bytes 524304 | tf_op jit(solution)/shard_map/psum | solution.py:56
  672.9 1.7 multiply_reduce_fusion.1
  675.1 10.4 %fusion.9 = f32[8,128,16,128]{3,1,2,0:T(8,128)S(1)} fusion(f32[8,128,128,1]{2,1,3,0:T(8,128)S(1)} %bitcast.85, f32[8,16,128,128]{3,2,1,0:T(8,128)} %bitcast.72, pred[8,16]{1,0:T(8,128)(4,1)S(1)} %compare_and_fusion), kind=kOutput, calls=%fused_computation.14 | convolution fusion | flops 3223322624 | bytes 17301632 | tf_op jit(solution)/shard_map/bkjr,bur->bkuj/dot_general | solution.py:13
  685.4 12.7 %fusion = f32[8,128,128,1]{2,1,3,0:T(8,128)S(1)} fusion(f32[8,16,128,128]{3,2,1,0:T(8,128)} %param.5, f32[8,128,16,128]{3,1,2,0:T(8,128)S(1)} %fusion.9, f32[8,16,128,128]{3,2,1,0:T(8,128)} %bitcast.73, pred[8,16]{1,0:T(8,128)(4,1)S(1)} %compare_and_fusion), kind=kOutput, calls=%fused_computation.2 | convolution fusion | flops 3225419776 | bytes 25690240 | tf_op jit(solution)/shard_map/bkuj,bkjr->bur/dot_general | solution.py:14
  699.2 138.0 %all-reduce.13.cloned.1.call-done = f32[1024,128]{0,1:T(8,128)} async-done(((f32[1024,128]{0,1:T(8,128)}), f32[1024,128]{0,1:T(8,128)}) %all-reduce.13.cloned.1.call-update) | async-done | bytes 524304 | tf_op jit(solution)/shard_map/psum | solution.py:56
  837.2 1.7 fusion.47
  (39 shorter events, 6.9 us)
Async XLA Ops:
  6.5 59.6 %all-gather.3.cloned.1.call-start = ((), (), s32[]{:S(2)}) async-start(), calls=%async_computation.4 | async-start | bytes 2228224 | tf_op jit(solution)/shard_map/all_gather | solution.py:41
  7.3 191.6 %all-reduce.7.cloned.1.call-start = ((), (), s32[]{:S(2)}) async-start(), calls=%async_computation | async-start | bytes 131072 | tf_op jit(solution)/shard_map/psum | solution.py:40
  9.3 334.6 %all-reduce.15.cloned.1.call-start = ((), (), s32[]{:S(2)}) async-start(), calls=%async_computation.5 | async-start | bytes 2228224 | tf_op jit(solution)/shard_map/psum | solution.py:40
  66.1 6.0 copy-start.1
  72.1 11.9 %copy-start = (f32[128,128,128]{2,1,0:T(8,128)S(1)}, f32[128,128,128]{2,1,0:T(8,128)}, u32[]{:S(2)}) copy-start(f32[128,128,128]{2,1,0:T(8,128)} %gather_fusion) | copy-start | bytes 25165828
  198.9 309.5 %all-reduce.9.cloned.1.call-start = ((), (), s32[]{:S(2)}) async-start(), calls=%async_computation.1 | async-start | bytes 1048576 | tf_op jit(solution)/shard_map/psum | solution.py:56
  356.7 151.7 %copy-start.2 = (f32[128,128]{1,0:T(8,128)S(1)}, f32[128,128]{1,0:T(8,128)}, u32[]{:S(2)}) copy-start(f32[128,128]{1,0:T(8,128)} %get-tuple-element.7) | copy-start | bytes 196612
  370.6 302.3 %all-reduce.11.cloned.1.call-start = ((), (), s32[]{:S(2)}) async-start(), calls=%async_computation.2 | async-start | bytes 1048576 | tf_op jit(solution)/shard_map/psum | solution.py:56
  534.7 302.5 %all-reduce.13.cloned.1.call-start = ((), (), s32[]{:S(2)}) async-start(), calls=%async_computation.3 | async-start | bytes 1048576 | tf_op jit(solution)/shard_map/psum | solution.py:56
Sparse Core Ops, SparseCore 0:
  10.0 56.0 all-gather.2
  68.7 130.0 all-reduce.6
  201.7 142.1 all-reduce.14
  370.7 137.6 all-reduce.8
  534.8 138.0 all-reduce.10
  699.3 137.8 all-reduce.12
